TPU v7x, 512 devices: a whole 4x8x8 slice. The times are simulated.
512 devices in a mesh: row: 64 (over z, y_lo, x), col: 8 (over y_hi, core).
Axes of the slice: x: 4, y: 8 (y_hi: 4, y_lo: 2; y = y_hi * 2 + y_lo), z: 8, core: 2. Of those that a mesh axis runs over, the one named last changes fastest.
Arguments:
- trailing: bfloat16 [32768, 4096], P('row', 'col'), may hold values from -6 to 6
- u_factor: bfloat16 [64, 8, 512, 256], P('row', 'col'), may hold values from -0.07861328 to 0.07861328
- w_factor: bfloat16 [64, 8, 512, 256], P('row', 'col'), may hold values from -4.1875 to 4.1875
- diag_inverse: bfloat16 [8, 512, 512], P('col'), as said below
- ranks: int32 [64, 8], P('row', 'col'), may hold values from 32 to 256, as said below
- col_rows: int32 [8], replicated, may hold values from 0 to 63, as said below
Outputs:
- updated: float32 [32768, 4096], P('row', 'col')
Inputs may be any that keep to these rules, and one draw needn't show every extreme that they name: `ranks`: each tile's rank; some tile has rank 256 and some has rank 256 // 8. `col_rows`: distinct tile rows. `diag_inverse`: lower triangular, diagonal between 0.5 and 2.
All inputs are finite; a program needn't handle non-finite values.
Results may differ from a plain program's by a relative error of at most 0.0047.
Values may be sent and summed in bfloat16 or wider, within the bound.
A program may use at most 64 MiB of HBM per device.

v0:
```python
import jax
import jax.numpy as jnp
from jax import lax
from jax.sharding import PartitionSpec as P


def spread(block, axis, source):
    block = jnp.where(lax.axis_index(axis) == source, block, jnp.zeros_like(block))
    return lax.psum(block, axis)


def panel_update(left_rows, right_rows, left_cols, right_cols):
    core = jnp.einsum(
        "ktr,kts->krs", right_rows, right_cols, preferred_element_type=jnp.float32
    ).astype(jnp.bfloat16)
    mixed = jnp.einsum("ktr,krs->kts", left_rows, core, preferred_element_type=jnp.float32).astype(
        jnp.bfloat16
    )
    return jnp.einsum("kts,kus->tu", mixed, left_cols, preferred_element_type=jnp.float32)


def local(trailing, u_factor, w_factor, diag_inverse, ranks, col_rows):
    rank_max = w_factor.shape[3]
    product = jnp.einsum(
        "ktu,kur->ktr", diag_inverse, w_factor[0], preferred_element_type=jnp.float32
    )
    keep = jnp.arange(rank_max, dtype=jnp.int32)[None, :] < ranks[0][:, None]
    solved = jnp.where(keep[:, None, :], product.astype(jnp.bfloat16), jnp.zeros((), jnp.bfloat16))
    paired = jnp.stack([u_factor[0], solved])
    gathered = lax.all_gather(paired, "col", axis=1, tiled=True)
    root = col_rows[lax.axis_index("col")]
    base = trailing.astype(jnp.float32)
    column = spread(gathered, "row", root)
    result = base - panel_update(gathered[0], gathered[1], column[0], column[1])
    return result


def solution(mesh):
    placed = (
        P("row", "col"),
        P("row", "col", None, None),
        P("row", "col", None, None),
        P("col", None, None),
        P("row", "col"),
        P(),
    )
    return jax.shard_map(
        local, mesh=mesh, in_specs=placed, out_specs=P("row", "col"), check_vma=False
    )
```

profile of v0, /device:TPU:20, one launch (start us, length us, event | category | flops | bytes accessed | tf_op | source)
XLA Modules:
  0.0 713.0 jit_solution(2069251097134000312)
XLA Ops:
  6.5 0.0 copy-start
  6.5 0.0 all-gather.2.cloned.1.call-start
  7.3 0.3 copy-done
  7.6 1.2 fusion.12
  8.8 1.8 pad_maximum_fusion
  10.6 0.0 all-gather.2.cloned.1.call-update
  10.7 0.0 all-reduce.2.cloned.1.call-start
  10.7 1.3 dynamic_slice.3
  12.6 54.2 %all-gather.2.cloned.1.call-done = bf16[2,8,512,256]{3,2,1,0:T(8,128)(2,1)} async-done(((bf16[2,1,512,256]{3,2,1,0:T(8,128)(2,1)}), bf16[2,8,512,256]{3,2,1,0:T(8,128)(2,1)}) %all-gather.2.cloned.1.call-update) | async-done | bytes 4194320 | tf_op jit(solution)/shard_map/all_gather | solution.py:30
  66.8 2.2 broadcast_select_fusion
  69.1 0.0 all-reduce.2.cloned.1.call-update
  69.1 0.0 copy-start.1
  69.1 629.0 %all-reduce.2.cloned.1.call-done = bf16[2,8,512,256]{3,2,1,0:T(8,128)(2,1)} async-done(((bf16[2,8,512,256]{3,2,1,0:T(8,128)(2,1)}), bf16[2,8,512,256]{3,2,1,0:T(8,128)(2,1)}) %all-reduce.2.cloned.1.call-update) | async-done | bytes 4194320 | tf_op jit(solution)/shard_map/psum | solution.py:9
  698.1 3.0 fusion.4
  701.1 0.0 copy-done.1
  701.2 5.0 fusion.8
  (1 shorter events, 0.0 us)
Async XLA Ops:
  6.5 1.1 copy-start
  6.5 60.3 %all-gather.2.cloned.1.call-start = ((), (), s32[]{:S(2)}) async-start(), calls=%async_computation | async-start | bytes 4718592 | tf_op jit(solution)/shard_map/all_gather | solution.py:30
  10.7 687.5 %all-reduce.2.cloned.1.call-start = ((), (), s32[]{:S(2)}) async-start(), calls=%async_computation.1 | async-start | bytes 8388608 | tf_op jit(solution)/shard_map/psum | solution.py:9
  69.1 632.1 %copy-start.1 = (bf16[512,512]{1,0:T(8,128)(2,1)S(1)}, bf16[512,512]{1,0:T(8,128)(2,1)}, u32[]{:S(2)}) copy-start(bf16[512,512]{1,0:T(8,128)(2,1)} %param.6) | copy-start | bytes 1572868
Sparse Core Ops, SparseCore 0:
  10.8 55.9 all-gather.1
  69.7 628.3 all-reduce.1
where the time goes:
time: 714 us; the launch traced here: 713 us
  waiting for transfers between devices  683 us (96%)
  between operations  14.8 us (2%)
  matrix products  9.24 us (1%)
    psum x1, waiting for transfers between devices, spread(): return lax.psum(block, axis)  629 us
    all_gather x1, waiting for transfers between devices, local(): gathered = lax.all_gather(paired, 'col', axis=1, tiled=True)  54.2 us
  transfers between devices with their start and end apart: 2, of which 2 were waited for; matrix products, arithmetic and copies ran while one was open for 0% of the time, Pallas kernels for 0%

commit v1 on v0

--- a/solution.py
+++ b/solution.py
@@ -2,11 +2,6 @@
 import jax.numpy as jnp
 from jax import lax
 from jax.sharding import PartitionSpec as P
-
-
-def spread(block, axis, source):
-    block = jnp.where(lax.axis_index(axis) == source, block, jnp.zeros_like(block))
-    return lax.psum(block, axis)
 
 
 def panel_update(left_rows, right_rows, left_cols, right_cols):
@@ -20,18 +15,24 @@
 
 
 def local(trailing, u_factor, w_factor, diag_inverse, ranks, col_rows):
-    rank_max = w_factor.shape[3]
+    tile, rank_max = w_factor.shape[2:]
+    rows = lax.axis_size("row")
     product = jnp.einsum(
         "ktu,kur->ktr", diag_inverse, w_factor[0], preferred_element_type=jnp.float32
     )
     keep = jnp.arange(rank_max, dtype=jnp.int32)[None, :] < ranks[0][:, None]
     solved = jnp.where(keep[:, None, :], product.astype(jnp.bfloat16), jnp.zeros((), jnp.bfloat16))
-    paired = jnp.stack([u_factor[0], solved])
-    gathered = lax.all_gather(paired, "col", axis=1, tiled=True)
-    root = col_rows[lax.axis_index("col")]
+    paired = jnp.concatenate([u_factor[0], solved], axis=1)
+    pieces = paired.reshape(rows, 2 * tile // rows, rank_max)
+    spread = lax.all_to_all(pieces, "row", 0, 0, tiled=True)
+    chosen = jnp.take(spread, col_rows, axis=0)
+    mine = lax.all_to_all(chosen, "col", 0, 0, tiled=True)
+    column = lax.all_gather(mine, "row", axis=1, tiled=True)
+    gathered = lax.all_gather(paired, "col", axis=0, tiled=True)
     base = trailing.astype(jnp.float32)
-    column = spread(gathered, "row", root)
-    result = base - panel_update(gathered[0], gathered[1], column[0], column[1])
+    result = base - panel_update(
+        gathered[:, :tile], gathered[:, tile:], column[:, :tile], column[:, tile:]
+    )
     return result
 
 

time: 714 us -> 394 us (0.55)
  the two profiles are of different devices: /device:TPU:20 before, /device:TPU:16 now
where the time goes in v1:
time: 394 us; the launch traced here: 393 us
  waiting for transfers between devices  337 us (86%)
  starting transfers between devices  15 us (4%)
  blocking collectives  14.3 us (4%)
  between operations  14.2 us (4%)
  matrix products  9.26 us (2%)
    all_gather x1, waiting for transfers between devices, local(): column = lax.all_gather(mine, 'row', axis=1, tiled=True)  310 us
    all_to_all x1, waiting for transfers between devices, local(): spread = lax.all_to_all(pieces, 'row', 0, 0, tiled=True)  17.2 us
    all_to_all x1, starting transfers between devices, local(): spread = lax.all_to_all(pieces, 'row', 0, 0, tiled=True)  14.9 us
    all_to_all x1, blocking collectives, local(): mine = lax.all_to_all(chosen, 'col', 0, 0, tiled=True)  14.3 us
    all_gather x1, waiting for transfers between devices, local(): gathered = lax.all_gather(paired, 'col', axis=0, tiled=True)  9.15 us
  transfers between devices with their start and end apart: 3, of which 3 were waited for; matrix products, arithmetic and copies ran while one was open for 0% of the time, Pallas kernels for 0%

profile of v1, /device:TPU:16, one launch (start us, length us, event | category | flops | bytes accessed | tf_op | source)
XLA Modules:
  0.0 393.4 jit_solution(8181923480299634391)
XLA Ops:
  6.5 0.0 copy-start
  6.5 0.0 all-gather.3.cloned.1.call-start
  7.3 0.3 copy-done
  7.6 1.2 fusion.32
  8.8 1.8 pad_maximum_fusion
  10.6 0.0 copy-start.1
  10.6 0.0 all-gather.3.cloned.1.call-update
  10.7 14.9 %all-to-all-start = ((bf16[64,16,256]{2,1,0:T(8,128)(2,1)}), bf16[64,16,256]{2,1,0:T(8,128)(2,1)S(1)}, u32[]{:S(2)}, u32[]{:S(2)}) async-start(bf16[64,16,256]{2,1,0:T(8,128)(2,1)} %bitcast.17), calls=%async_computation | async-start | bytes 1048576 | tf_op jit(solution)/shard_map/all_to_all | solution.py:27
  25.6 0.0 all-gather.5.cloned.1.call-start
  25.6 0.7 compare_select_fusion
  26.3 0.7 compare_and_fusion
  27.0 17.2 %all-to-all-done = bf16[64,16,256]{2,1,0:T(8,128)(2,1)S(1)} async-done(((bf16[64,16,256]{2,1,0:T(8,128)(2,1)}), bf16[64,16,256]{2,1,0:T(8,128)(2,1)S(1)}, u32[]{:S(2)}, u32[]{:S(2)}) %all-to-all-start) | async-done | bytes 524320 | tf_op jit(solution)/shard_map/all_to_all | solution.py:27
  44.2 0.5 gather_fusion
  44.8 0.1 broadcast_select_fusion
  44.9 14.3 %all_to_all.10 = bf16[8,16,256]{2,1,0:T(8,128)(2,1)} all-to-all(bf16[8,16,256]{2,1,0:T(8,128)(2,1)S(1)} %broadcast_select_fusion), channel_id=1, replica_groups=mesh['row'=64,'col'=8] {'col'}, dimensions={0} | all-to-all | bytes 131072 | tf_op jit(solution)/shard_map/all_to_all | solution.py:29
  59.2 0.0 all-gather.5.cloned.1.call-update
  59.2 9.1 %all-gather.3.cloned.1.call-done = bf16[8,1024,256]{2,1,0:T(8,128)(2,1)} async-done(((bf16[1,1024,256]{2,1,0:T(8,128)(2,1)}), bf16[8,1024,256]{2,1,0:T(8,128)(2,1)}) %all-gather.3.cloned.1.call-update) | async-done | bytes 4194320 | tf_op jit(solution)/shard_map/all_gather | solution.py:31
  68.4 310.1 %all-gather.5.cloned.1.call-done = bf16[8,1024,256]{2,1,0:T(8,128)(2,1)} async-done(((bf16[8,16,256]{2,1,0:T(8,128)(2,1)}), bf16[8,1024,256]{2,1,0:T(8,128)(2,1)}) %all-gather.5.cloned.1.call-update) | async-done | bytes 4194320 | tf_op jit(solution)/shard_map/all_gather | solution.py:30
  378.5 3.0 fusion.12
  381.5 0.0 copy-done.1
  381.5 5.0 %fusion.24 = f32[512,512]{1,0:T(8,128)} fusion(bf16[8,1024,256]{2,1,0:T(8,128)(2,1)} %all-gather.5.cloned.1.call-done, bf16[8,256,256]{2,1,0:T(8,128)(2,1)S(1)} %fusion.12, bf16[8,1024,256]{2,1,0:T(8,128)(2,1)} %all-gather.3.cloned.1.call-done, bf16[512,512]{1,0:T(8,128)(2,1)S(1)} %copy-done.1), kind=kOutput, calls=%fused_computation.11 | convolution fusion | flops 1612185600 | bytes 6815744 | tf_op jit(solution)/shard_map/kts,kus->tu/dot_general | solution.py:14
  (2 shorter events, 0.0 us)
Async XLA Ops:
  6.5 1.1 copy-start
  6.5 61.8 %all-gather.3.cloned.1.call-start = ((), (), s32[]{:S(2)}) async-start(), calls=%async_computation.2 | async-start | bytes 4718592 | tf_op jit(solution)/shard_map/all_gather | solution.py:31
  10.6 370.9 %copy-start.1 = (bf16[512,512]{1,0:T(8,128)(2,1)S(1)}, bf16[512,512]{1,0:T(8,128)(2,1)}, u32[]{:S(2)}) copy-start(bf16[512,512]{1,0:T(8,128)(2,1)} %param.6) | copy-start | bytes 1572868
  10.7 33.6 %all-to-all-start = ((bf16[64,16,256]{2,1,0:T(8,128)(2,1)}), bf16[64,16,256]{2,1,0:T(8,128)(2,1)S(1)}, u32[]{:S(2)}, u32[]{:S(2)}) async-start(bf16[64,16,256]{2,1,0:T(8,128)(2,1)} %bitcast.17), calls=%async_computation | async-start | bytes 1048576 | tf_op jit(solution)/shard_map/all_to_all | solution.py:27
  25.6 352.9 %all-gather.5.cloned.1.call-start = ((), (), s32[]{:S(2)}) async-start(), calls=%async_computation.3 | async-start | bytes 4259840 | tf_op jit(solution)/shard_map/all_gather | solution.py:30
Sparse Core Ops, SparseCore 0:
  10.8 57.5 all-gather.2
  70.5 307.9 all-gather.4

commit v2 on v0

v2 whole, which is shorter than its diff:
```python
import jax
import jax.numpy as jnp
from jax import lax
from jax.experimental import pallas as pl
from jax.experimental.pallas import tpu as pltpu
from jax.sharding import PartitionSpec as P

MESH = pl.DeviceIdType.MESH
ROWS, COLS = 64, 8
NX, NY, NZ, NH = 4, 2, 8, 4
TILE, RANK = 512, 256
BOTH = 2 * TILE
PIECE = BOTH // ROWS
STEP = NY * PIECE
SLAB = NX * STEP
FIRST = 3


def aligned(value, factor):
    return pl.multiple_of(value * factor, factor)


def kernel(
    pairs, ranks, trailing, u_ref, w_ref, inverse, out,
    mine, theirs, landed, picked,
    spread_sem, place_sem, ring_sems, x_sems, z_sems, wide_x_sems, wide_z_sems,
):
    row, col = lax.axis_index("row"), lax.axis_index("col")
    z, y, x = row // (NX * NY), (row // NX) % NY, row % NX
    h, core = col // 2, col % 2

    def at(new_z, new_y, new_x):
        return (new_z * NY + new_y) * NX + new_x

    def piece_of(other):
        return (other // (NX * NY)) * (NX * NY) + (other % NX) * NY + (other // NX) % NY

    partner = at(z, 1 - y, x)

    barrier = pltpu.get_barrier_semaphore()

    @pl.loop(1, ROWS)
    def _(d):
        pl.semaphore_signal(barrier, inc=1, device_id=((row + d) % ROWS, col), device_id_type=MESH)

    @pl.loop(1, COLS)
    def _(d):
        other = (col + d) % COLS
        pl.semaphore_signal(barrier, inc=1, device_id=(row, other), device_id_type=MESH)
        pl.semaphore_signal(barrier, inc=1, device_id=(partner, other), device_id_type=MESH)

    product = jnp.dot(inverse[0], w_ref[0, 0], preferred_element_type=jnp.float32)
    lane = lax.broadcasted_iota(jnp.int32, (TILE, RANK), 1)
    solved = jnp.where(lane < ranks[0, 0], product, 0.0).astype(jnp.bfloat16)
    mine[col, TILE:, :] = solved
    mine[col, :TILE, :] = u_ref[0, 0]

    pl.semaphore_wait(barrier, ROWS - 1 + 2 * (COLS - 1))

    sent = []

    def send(source, target, send_sem, recv_sem, to_row, to_col):
        copy = pltpu.make_async_remote_copy(
            src_ref=source, dst_ref=target, send_sem=send_sem, recv_sem=recv_sem,
            device_id=(to_row, to_col), device_id_type=MESH,
        )
        copy.start()
        sent.append(copy)

    def arrived(target, sem):
        pltpu.make_async_copy(target, target, sem).wait()

    own_piece = aligned(piece_of(row), PIECE)
    landed[row] = mine[col, pl.ds(own_piece, PIECE), :]

    @pl.loop(1, ROWS)
    def _(d):
        other = (row + d) % ROWS
        pltpu.make_async_remote_copy(
            src_ref=mine.at[col, pl.ds(aligned(piece_of(other), PIECE), PIECE), :],
            dst_ref=landed.at[row],
            send_sem=spread_sem.at[0], recv_sem=spread_sem.at[1],
            device_id=(other, col), device_id_type=MESH,
        ).start()

    right, left = ((h + 1) % NH) * 2 + core, ((h + NH - 1) % NH) * 2 + core
    across, twin = ((h + 2) % NH) * 2 + core, col + 1 - 2 * core
    halves = (pl.ds(0, TILE), pl.ds(TILE, TILE))
    count = [0]

    def pass_on(panel, half, to, slot):
        block = mine.at[panel, halves[half], :]
        send(block, block, ring_sems.at[0, count[0]], ring_sems.at[1, slot], row, to)
        count[0] += 1

    def ring_arrived(panel, half, slot):
        arrived(mine.at[panel, halves[half], :], ring_sems.at[1, slot])

    pass_on(col, 0, right, 0)
    pass_on(col, 1, left, 3)
    pass_on(col, 1, right, 1)
    pass_on(col, 0, left, 2)
    pass_on(col, 0, twin, 6)
    pass_on(col, 1, twin, 7)

    arrived(landed.at[pl.ds(0, ROWS - 1)], spread_sem.at[1])
    chosen = picked
    spot = (col, pl.ds(own_piece, PIECE), slice(None))
    for c in range(COLS):
        chosen[c] = landed[pairs[c]]

    @pl.loop(1, COLS)
    def _(d):
        other = (col + d) % COLS
        for to_row in (row, partner):
            pltpu.make_async_remote_copy(
                src_ref=chosen.at[other], dst_ref=theirs.at[spot],
                send_sem=place_sem.at[0], recv_sem=place_sem.at[1],
                device_id=(to_row, other), device_id_type=MESH,
            ).start()

    pltpu.make_async_remote_copy(
        src_ref=chosen.at[col], dst_ref=theirs.at[spot],
        send_sem=place_sem.at[0], recv_sem=place_sem.at[1],
        device_id=(partner, col), device_id_type=MESH,
    ).start()
    theirs[spot] = chosen[col]
    arrived(landed.at[pl.ds(0, 2 * COLS - 1)], place_sem.at[1])

    few, many = pl.ds(0, FIRST), pl.ds(FIRST, COLS - FIRST)
    x_side = (at(z, y, (x + 1) % NX), at(z, y, (x + NX - 1) % NX))
    z_side = (at((z + 1) % NZ, y, x), at((z + NZ - 1) % NZ, y, x))

    def x_from(way, hops):
        return (x + NX - hops) % NX if way == 0 else (x + hops) % NX

    def z_from(way, hops):
        return (z + NZ - hops) % NZ if way == 0 else (z + hops) % NZ

    def small(panels, from_z, from_x, half=None):
        start = from_z * SLAB + from_x * STEP
        if half is None:
            return theirs.at[panels, pl.ds(pl.multiple_of(start, STEP), STEP), :]
        start = pl.multiple_of(start + half * PIECE, PIECE)
        return theirs.at[panels, pl.ds(start, PIECE), :]

    def large(panel, from_z, half=None):
        if half is None:
            return theirs.at[panel, pl.ds(aligned(from_z, SLAB), SLAB), :]
        return theirs.at[panel, pl.ds(aligned(from_z * 2 + half, SLAB // 2), SLAB // 2), :]

    def send_x(block, way, slot):
        send(block, block, x_sems.at[0, way, slot], x_sems.at[1, way, slot], x_side[way], col)

    def send_z(block, way, panel, slot):
        sems = z_sems
        send(block, block, sems.at[0, way, panel, slot], sems.at[1, way, panel, slot], z_side[way], col)

    def send_wide_z(block, way, slot):
        sems = wide_z_sems
        send(block, block, sems.at[0, way, slot], sems.at[1, way, slot], z_side[way], col)

    def send_wide_x(block, way, slot):
        sems = wide_x_sems
        send(block, block, sems.at[0, way, slot], sems.at[1, way, slot], x_side[way], col)

    ways = (0, 1)
    order = [(0, 0)] + [(w, s) for s in (1, 2, 3) for w in ways] + [(0, 4)]

    def place_z(entry):
        return z_from(*entry)

    for w in ways:
        send_x(small(few, z, x), w, 0)
    for w in ways:
        send_wide_z(small(many, z, x), w, 0)
    for w in ways:
        send_wide_x(small(many, z, x), w, 0)

    def wide_step(step):
        for w in ways:
            if step < 4:
                arrived(small(many, z_from(w, step), x), wide_z_sems.at[1, w, step - 1])
            else:
                arrived(small(many, z_from(w, step), x, w), wide_z_sems.at[1, w, step - 1])
            if step < 3:
                send_wide_z(small(many, z_from(w, step), x), w, step)
            elif step == 3:
                send_wide_z(small(many, z_from(w, step), x, w), w, step)
        if step < 4:
            for w in ways:
                slot = order.index((w, step))
                for v in ways:
                    send_wide_x(small(many, z_from(w, step), x), v, slot)
        else:
            for v in ways:
                send_wide_x(small(many, z_from(0, 4), x), v, 7)

    def second_hop(slots):
        for slot in slots:
            from_z = place_z(order[slot])
            for v in ways:
                arrived(small(many, from_z, x_from(v, 1)), wide_x_sems.at[1, v, slot])
            v = slot % 2
            send_wide_x(small(many, from_z, x_from(v, 1)), v, 8 + slot // 2)

    for w in ways:
        arrived(small(few, z, x_from(w, 1)), x_sems.at[1, w, 0])
        send_x(small(few, z, x_from(w, 1), w), w, 1)
    wide_step(1)
    for w in ways:
        arrived(small(few, z, x_from(w, 2), w), x_sems.at[1, w, 1])
    for k in range(FIRST):
        for w in ways:
            send_z(large(k, z), w, k, 0)
    wide_step(2)
    second_hop([0])
    ring_arrived(left, 0, 0)
    pass_on(left, 0, right, 4)
    ring_arrived(right, 1, 3)
    pass_on(right, 1, left, 5)
    wide_step(3)
    for k in range(FIRST):
        for w in ways:
            arrived(large(k, z_from(w, 1)), z_sems.at[1, w, k, 0])
            send_z(large(k, z_from(w, 1)), w, k, 1)
    second_hop([1, 2])
    wide_step(4)
    for k in range(FIRST):
        for w in ways:
            arrived(large(k, z_from(w, 2)), z_sems.at[1, w, k, 1])
            send_z(large(k, z_from(w, 2)), w, k, 2)
    second_hop([3, 4])
    pass_on(left, 0, twin, 8)
    pass_on(right, 1, twin, 11)
    ring_arrived(left, 1, 1)
    pass_on(left, 1, twin, 9)
    ring_arrived(right, 0, 2)
    pass_on(right, 0, twin, 10)
    for k in range(FIRST):
        for w in ways:
            arrived(large(k, z_from(w, 3)), z_sems.at[1, w, k, 2])
            send_z(large(k, z_from(w, 3), w), w, k, 3)
    second_hop([5, 6])
    second_hop([7])
    ring_arrived(across, 0, 4)
    pass_on(across, 0, twin, 12)
    ring_arrived(across, 1, 5)
    pass_on(across, 1, twin, 13)
    for k in range(FIRST):
        for w in ways:
            arrived(large(k, z_from(w, 4), w), z_sems.at[1, w, k, 3])
    for slot in range(8):
        v = slot % 2
        from_z = place_z(order[slot])
        arrived(small(many, from_z, x_from(v, 2)), wide_x_sems.at[1, v, 8 + slot // 2])
    flip = 1 - 2 * core
    for panel, base in ((twin, 6), (left + flip, 8), (right + flip, 10), (across + flip, 12)):
        ring_arrived(panel, 0, base)
        ring_arrived(panel, 1, base + 1)

    out[...] = trailing[...].astype(jnp.float32)

    @pl.loop(0, COLS)
    def _(k):
        middle = lax.dot_general(
            mine[k, TILE:, :], theirs[k, TILE:, :], (((0,), (0,)), ((), ())),
            preferred_element_type=jnp.float32,
        ).astype(jnp.bfloat16)
        mixed = jnp.dot(
            mine[k, :TILE, :], middle, preferred_element_type=jnp.float32
        ).astype(jnp.bfloat16)
        out[...] -= lax.dot_general(
            mixed, theirs[k, :TILE, :], (((1,), (1,)), ((), ())),
            preferred_element_type=jnp.float32,
        )

    for copy in sent:
        copy.wait_send()
    arrived(landed.at[pl.ds(0, ROWS - 1)], spread_sem.at[0])
    arrived(landed.at[pl.ds(0, 2 * COLS - 1)], place_sem.at[0])


def local(trailing, u_factor, w_factor, diag_inverse, ranks, col_rows):
    vmem, smem = pl.BlockSpec(memory_space=pltpu.VMEM), pl.BlockSpec(memory_space=pltpu.SMEM)
    sems = pltpu.SemaphoreType.DMA
    return pl.pallas_call(
        kernel,
        out_shape=jax.ShapeDtypeStruct((TILE, TILE), jnp.float32),
        in_specs=[smem, smem, vmem, vmem, vmem, vmem],
        out_specs=vmem,
        scratch_shapes=[
            pltpu.VMEM((COLS, BOTH, RANK), jnp.bfloat16),
            pltpu.VMEM((COLS, BOTH, RANK), jnp.bfloat16),
            pltpu.VMEM((ROWS, PIECE, RANK), jnp.bfloat16),
            pltpu.VMEM((COLS, PIECE, RANK), jnp.bfloat16),
            sems((2,)),
            sems((2,)),
            sems((2, 14)),
            sems((2, 2, 2)),
            sems((2, 2, FIRST, 4)),
            sems((2, 2, 12)),
            sems((2, 2, 4)),
        ],
        compiler_params=pltpu.CompilerParams(
            collective_id=0, has_side_effects=True, vmem_limit_bytes=40 * 2**20
        ),
    )(col_rows, ranks, trailing, u_factor, w_factor, diag_inverse)


def solution(mesh):
    placed = (
        P("row", "col"),
        P("row", "col", None, None),
        P("row", "col", None, None),
        P("col", None, None),
        P("row", "col"),
        P(),
    )
    return jax.shard_map(
        local, mesh=mesh, in_specs=placed, out_specs=P("row", "col"), check_vma=False
    )
```

time: 714 us -> 93 us (0.13)
  the two profiles are of different devices: /device:TPU:20 before, /device:TPU:1 now
where the time goes in v2:
time: 93 us; the launch traced here: 91.6 us
  Pallas kernels  86 us (92%)
  local copies, waits for them, and re-layouts  4.95 us (5%)
    pallas_call x1, Pallas kernels, local(): pl.pallas_call(kernel, out_shape=jax.ShapeDtypeStruct((TILE, TILE), jnp.f...  86 us
    unnamed x11, local copies, waits for them, and re-layouts  4.95 us

profile of v2, /device:TPU:1, one launch (start us, length us, event | category | flops | bytes accessed | tf_op | source)
XLA Modules:
  0.0 91.6 jit_solution(12030264728478423563)
XLA Ops:
  0.0 0.0 copy-start.4
  0.7 0.0 copy-done.4
  0.7 0.0 copy-start
  0.7 1.0 %copy-done = bf16[512,512]{1,0:T(8,128)(2,1)S(1)} copy-done((bf16[512,512]{1,0:T(8,128)(2,1)S(1)}, bf16[512,512]{1,0:T(8,128)(2,1)}, u32[]{:S(2)}) %copy-start) | copy-done | bytes 524312
  1.7 0.0 copy-start.1
  1.7 1.0 %copy-done.1 = bf16[1,512,512]{2,1,0:T(8,128)(2,1)S(1)} copy-done((bf16[1,512,512]{2,1,0:T(8,128)(2,1)S(1)}, bf16[1,512,512]{2,1,0:T(8,128)(2,1)}, u32[]{:S(2)}) %copy-start.1) | copy-done | bytes 524312
  2.8 0.0 copy-start.2
  2.8 0.9 %copy-done.2 = bf16[1,1,512,256]{3,2,1,0:T(8,128)(2,1)S(1)} copy-done((bf16[1,1,512,256]{3,2,1,0:T(8,128)(2,1)S(1)}, bf16[1,1,512,256]{3,2,1,0:T(8,128)(2,1)}, u32[]{:S(2)}) %copy-start.2) | copy-done | bytes 262168
  3.7 0.0 copy-start.3
  3.7 0.9 %copy-done.3 = bf16[1,1,512,256]{3,2,1,0:T(8,128)(2,1)S(1)} copy-done((bf16[1,1,512,256]{3,2,1,0:T(8,128)(2,1)S(1)}, bf16[1,1,512,256]{3,2,1,0:T(8,128)(2,1)}, u32[]{:S(2)}) %copy-start.3) | copy-done | bytes 262168
  4.7 86.0 %shard_map.64 = f32[512,512]{1,0:T(8,128)S(1)} custom-call(s32[8]{0:T(128)S(1)} %copy-done.4, s32[1,1]{1,0:T(1,128)S(6)} %copy.8.ranks, bf16[512,512]{1,0:T(8,128)(2,1)S(1)} %copy-done, bf16[1,1,512,256]{3,2,1,0:T(8,128)(2,1)S(1)} %copy-done.2, bf16[1,1,512,256]{3,2,1,0:T(8,128)(2,1)S(1)} %copy-done.3, bf16[1,512,512]{2,1,0:T(8,128)(2,1)S(1)} %copy-done.1), custom_call_target="tpu_custom_call" | custom-call | tf_op jit(solution)/shard_map/pallas_call | solution.py:287
  90.6 1.0 %copy.9 = f32[512,512]{1,0:T(8,128)} copy(f32[512,512]{1,0:T(8,128)S(1)} %shard_map.64) | data formatting | bytes 2097152
Async XLA Ops:
  0.0 0.7 copy-start.4
  0.7 1.0 %copy-start = (bf16[512,512]{1,0:T(8,128)(2,1)S(1)}, bf16[512,512]{1,0:T(8,128)(2,1)}, u32[]{:S(2)}) copy-start(bf16[512,512]{1,0:T(8,128)(2,1)} %trailing.1) | copy-start | bytes 1572868
  1.7 1.0 %copy-start.1 = (bf16[1,512,512]{2,1,0:T(8,128)(2,1)S(1)}, bf16[1,512,512]{2,1,0:T(8,128)(2,1)}, u32[]{:S(2)}) copy-start(bf16[1,512,512]{2,1,0:T(8,128)(2,1)} %inverse.1) | copy-start | bytes 1572868
  2.8 0.9 %copy-start.2 = (bf16[1,1,512,256]{3,2,1,0:T(8,128)(2,1)S(1)}, bf16[1,1,512,256]{3,2,1,0:T(8,128)(2,1)}, u32[]{:S(2)}) copy-start(bf16[1,1,512,256]{3,2,1,0:T(8,128)(2,1)} %u_ref.1) | copy-start | bytes 786436
  3.7 0.9 %copy-start.3 = (bf16[1,1,512,256]{3,2,1,0:T(8,128)(2,1)S(1)}, bf16[1,1,512,256]{3,2,1,0:T(8,128)(2,1)}, u32[]{:S(2)}) copy-start(bf16[1,1,512,256]{3,2,1,0:T(8,128)(2,1)} %w_ref.1) | copy-start | bytes 786436

commit v3 on v0

v3 whole, which is shorter than its diff:
```python
import jax
import jax.numpy as jnp
from jax import lax
from jax.experimental import pallas as pl
from jax.experimental.pallas import tpu as pltpu
from jax.sharding import PartitionSpec as P

MESH = pl.DeviceIdType.MESH
ROWS, COLS = 64, 8
NX, NY, NZ, NH = 4, 2, 8, 4
TILE, RANK = 512, 256
LANES = RANK // NY
STEP = TILE // (NX * NZ)
SLAB = NX * STEP
WAYS = (0, 1)
GROUPS = ((0, 3), (3, 2), (5, 3))
PLAN = (
    0, 1, 3, 5, 5, 1, 1, 3, 3, 0, 2, 4, 1, 1, 2, 2, 3, 3, 5, 5, 4, 0, 0, 4, 0, 0, 0, 0, 2, 1, 1, 2,
    3, 3, 4, 0, 0, 4, 0, 0, 2, 0, 0, 2, 1, 3, 5, 5, 4, 0, 0, 4, 0, 0, 0, 0, 2, 4, 5, 0, 2, 4,
)
ORDER = [(0, 0)] + [(w, s) for s in (1, 2, 3) for w in WAYS] + [(0, 4)]


def kernel(
    pairs, ranks, trailing, u_ref, w_ref, inverse_ref, out,
    mine, theirs, landed, picked, base, w, inverse,
    load_sems, own_sems, spread_sems, place_sems, ring_sems,
    x_sems, z_sems, wide_x_sems, wide_z_sems,
):
    row, col = lax.axis_index("row"), lax.axis_index("col")
    z, y, x = row // (NX * NY), (row // NX) % NY, row % NX
    h, core = col // 2, col % 2

    def at(new_z, new_y, new_x):
        return (new_z * NY + new_y) * NX + new_x

    partner = at(z, 1 - y, x)

    loads = [
        pltpu.make_async_copy(source, target, load_sems.at[i])
        for i, (source, target) in enumerate((
            (inverse_ref.at[0], inverse),
            (w_ref.at[0, 0], w),
            (u_ref.at[0, 0], mine.at[col, 1]),
            (trailing, base),
        ))
    ]
    for load in loads:
        load.start()

    barrier = pltpu.get_barrier_semaphore()

    @pl.loop(1, ROWS)
    def _(d):
        pl.semaphore_signal(barrier, inc=1, device_id=((row + d) % ROWS, col), device_id_type=MESH)

    @pl.loop(1, COLS)
    def _(d):
        other = (col + d) % COLS
        pl.semaphore_signal(barrier, inc=1, device_id=(row, other), device_id_type=MESH)
        pl.semaphore_signal(barrier, inc=1, device_id=(partner, other), device_id_type=MESH)

    loads[0].wait()
    loads[1].wait()
    product = jnp.dot(inverse[...], w[...], preferred_element_type=jnp.float32)
    lane = lax.broadcasted_iota(jnp.int32, (TILE, RANK), 1)
    mine[col, 0] = jnp.where(lane < ranks[0, 0], product, 0.0).astype(jnp.bfloat16)
    loads[2].wait()

    pl.semaphore_wait(barrier, ROWS - 1 + 2 * (COLS - 1))

    sent = []

    def send(source, target, send_sem, recv_sem, to_row, to_col):
        copy = pltpu.make_async_remote_copy(
            src_ref=source, dst_ref=target, send_sem=send_sem, recv_sem=recv_sem,
            device_id=(to_row, to_col), device_id_type=MESH,
        )
        copy.start()
        sent.append(copy)

    def arrived(target, sem):
        pltpu.make_async_copy(target, target, sem).wait()

    def piece(other):
        place = (other // (NX * NY)) * NX + other % NX
        first = pl.multiple_of((other // NX) % NY * LANES, LANES)
        return mine.at[
            col, :, pl.ds(pl.multiple_of(place * STEP, STEP), STEP), pl.ds(first, LANES)
        ]

    own = pltpu.make_async_copy(piece(row), landed.at[row], own_sems.at[0])
    own.start()

    @pl.loop(1, ROWS)
    def _(d):
        other = (row + d) % ROWS
        pltpu.make_async_remote_copy(
            src_ref=piece(other), dst_ref=landed.at[row],
            send_sem=spread_sems.at[0], recv_sem=spread_sems.at[1],
            device_id=(other, col), device_id_type=MESH,
        ).start()

    right, left = ((h + 1) % NH) * 2 + core, ((h + NH - 1) % NH) * 2 + core
    across, twin = ((h + 2) % NH) * 2 + core, col + 1 - 2 * core
    count = [0]

    def pass_on(panel, part, to, slot):
        ref = mine.at[panel, part]
        send(ref, ref, ring_sems.at[0, count[0]], ring_sems.at[1, slot], row, to)
        count[0] += 1

    def ring_arrived(panel, part, slot):
        arrived(mine.at[panel, part], ring_sems.at[1, slot])

    pass_on(col, 0, right, 0)
    pass_on(col, 1, left, 3)

    own.wait()
    arrived(landed.at[pl.ds(0, ROWS - 1)], spread_sems.at[1])
    spot = theirs.at[
        :, col, pl.ds(pl.multiple_of((z * NX + x) * STEP, STEP), STEP),
        pl.ds(pl.multiple_of(y * LANES, LANES), LANES),
    ]
    for c in range(COLS):
        picked[c] = landed[pairs[c]]

    def place(to_row, to_col):
        pltpu.make_async_remote_copy(
            src_ref=picked.at[to_col], dst_ref=spot,
            send_sem=place_sems.at[0], recv_sem=place_sems.at[1],
            device_id=(to_row, to_col), device_id_type=MESH,
        ).start()

    @pl.loop(1, COLS)
    def _(d):
        place(row, (col + d) % COLS)
        place(partner, (col + d) % COLS)

    place(partner, col)
    stay = pltpu.make_async_copy(picked.at[col], spot, own_sems.at[1])
    stay.start()
    pass_on(col, 1, right, 1)
    pass_on(col, 0, left, 2)
    stay.wait()
    arrived(landed.at[pl.ds(0, 2 * COLS - 1)], place_sems.at[1])

    x_side = (at(z, y, (x + 1) % NX), at(z, y, (x + NX - 1) % NX))
    z_side = (at((z + 1) % NZ, y, x), at((z + NZ - 1) % NZ, y, x))
    x_far = at(z, y, (x + 2) % NX)

    def x_from(way, hops):
        return (x + NX - hops) % NX if way == 0 else (x + hops) % NX

    def z_from(way, hops):
        return (z + NZ - hops) % NZ if way == 0 else (z + hops) % NZ

    def part_of(half):
        return pl.ds(0, RANK) if half is None else pl.ds(half * LANES, LANES)

    def small(panels, from_z, from_x, half=None):
        start = pl.multiple_of(from_z * SLAB + from_x * STEP, STEP)
        return theirs.at[:, panels, pl.ds(start, STEP), part_of(half)]

    def large(panel, from_z, half=None):
        start = pl.multiple_of(from_z * SLAB, SLAB)
        return theirs.at[:, panel, pl.ds(start, SLAB), part_of(half)]

    def shift(ref, sems, to_row):
        send(ref, ref, sems[0], sems[1], to_row, col)

    def narrow(first, size):
        panels = pl.ds(first, size)

        def begin():
            for v in WAYS:
                shift(small(panels, z, x), x_sems_of(v, 0), x_side[v])
            for v in WAYS:
                shift(small(panels, z, x, v), x_sems_of(v, 1), x_far)

        def turn():
            for v in WAYS:
                arrived(small(panels, z, x_from(v, 1)), x_sems_of(v, 0)[1])
                arrived(small(panels, z, x_from(v, 2), v), x_sems_of(v, 1)[1])
            for k in range(size):
                for v in WAYS:
                    shift(large(first + k, z), z_sems_of(v, k, 0), z_side[v])

        def relay(step, k, v):
            def run():
                arrived(large(first + k, z_from(v, step)), z_sems_of(v, k, step - 1)[1])
                half = v if step == 3 else None
                shift(large(first + k, z_from(v, step), half), z_sems_of(v, k, step), z_side[v])

            return run

        def end():
            for k in range(size):
                for v in WAYS:
                    arrived(large(first + k, z_from(v, 4), v), z_sems_of(v, k, 3)[1])

        relays = [relay(s, k, v) for s in (1, 2, 3) for k in range(size) for v in WAYS]
        return [begin, turn, *relays, end]

    def x_sems_of(v, slot):
        return x_sems.at[0, v, slot], x_sems.at[1, v, slot]

    def z_sems_of(v, k, slot):
        return z_sems.at[0, v, k, slot], z_sems.at[1, v, k, slot]

    def wide(group, first, size):
        panels = pl.ds(first, size)

        def along_z(v, slot):
            return wide_z_sems.at[group, 0, v, slot], wide_z_sems.at[group, 1, v, slot]

        def along_x(v, slot):
            return wide_x_sems.at[group, 0, v, slot], wide_x_sems.at[group, 1, v, slot]

        def sideways(slot):
            for v in WAYS:
                shift(small(panels, z_from(*ORDER[slot]), x), along_x(v, slot), x_side[v])

        def begin():
            for v in WAYS:
                shift(small(panels, z, x), along_z(v, 0), z_side[v])
            sideways(0)

        def relay(step, v):
            def run():
                arrived(small(panels, z_from(v, step), x), along_z(v, step - 1)[1])
                half = v if step == 3 else None
                shift(small(panels, z_from(v, step), x, half), along_z(v, step), z_side[v])
                sideways(ORDER.index((v, step)))

            return run

        def last():
            for v in WAYS:
                arrived(small(panels, z_from(v, 4), x, v), along_z(v, 3)[1])
            sideways(7)

        def hop(slot):
            def run():
                from_z, v = z_from(*ORDER[slot]), slot % 2
                for u in WAYS:
                    arrived(small(panels, from_z, x_from(u, 1)), along_x(u, slot)[1])
                shift(small(panels, from_z, x_from(v, 1)), along_x(v, 8 + slot // 2), x_side[v])

            return run

        def end():
            for slot in range(8):
                v = slot % 2
                block = small(panels, z_from(*ORDER[slot]), x_from(v, 2))
                arrived(block, along_x(v, 8 + slot // 2)[1])

        relays = [relay(s, v) for s in (1, 2, 3) for v in WAYS]
        return [begin, *relays, last], [*[hop(slot) for slot in range(8)], end]

    def onward(panel, part, slot, to, new_slot):
        def run():
            ring_arrived(panel, part, slot)
            pass_on(panel, part, to, new_slot)

        return run

    def cross_left():
        pass_on(col, 0, twin, 6)
        pass_on(col, 1, twin, 7)
        pass_on(left, 0, twin, 8)
        ring_arrived(left, 1, 1)
        pass_on(left, 1, twin, 9)

    def cross_right():
        pass_on(right, 1, twin, 11)
        ring_arrived(right, 0, 2)
        pass_on(right, 0, twin, 10)

    def ring_end():
        flip = 1 - 2 * core
        for panel, slot in ((twin, 6), (left + flip, 8), (right + flip, 10), (across + flip, 12)):
            ring_arrived(panel, 0, slot)
            ring_arrived(panel, 1, slot + 1)

    ring = [
        onward(left, 0, 0, right, 4), onward(right, 1, 3, left, 5), cross_left, cross_right,
        onward(across, 0, 4, twin, 12), onward(across, 1, 5, twin, 13), ring_end,
    ]
    flows = [narrow(*GROUPS[0]), *wide(0, *GROUPS[1]), *wide(1, *GROUPS[2]), ring]
    flows = [iter(flow) for flow in flows]

    def work(first, size):
        @pl.loop(first, first + size)
        def _(k):
            middle = lax.dot_general(
                mine[k, 0], theirs[0, k], (((0,), (0,)), ((), ())),
                preferred_element_type=jnp.float32,
            ).astype(jnp.bfloat16)
            mixed = jnp.dot(
                mine[k, 1], middle, preferred_element_type=jnp.float32
            ).astype(jnp.bfloat16)
            out[...] -= lax.dot_general(
                mixed, theirs[1, k], (((1,), (1,)), ((), ())), preferred_element_type=jnp.float32
            )

    for flow in PLAN[:-1]:
        next(flows[flow])()
    loads[3].wait()
    out[...] = base[...].astype(jnp.float32)
    work(0, GROUPS[2][0])
    next(flows[PLAN[-1]])()
    work(*GROUPS[2])

    for copy in sent:
        copy.wait_send()
    arrived(landed.at[pl.ds(0, ROWS - 1)], spread_sems.at[0])
    arrived(landed.at[pl.ds(0, 2 * COLS - 1)], place_sems.at[0])


def local(trailing, u_factor, w_factor, diag_inverse, ranks, col_rows):
    vmem, smem = pl.BlockSpec(memory_space=pltpu.VMEM), pl.BlockSpec(memory_space=pltpu.SMEM)
    anywhere = pl.BlockSpec(memory_space=pl.ANY)
    sems, half = pltpu.SemaphoreType.DMA, jnp.bfloat16
    return pl.pallas_call(
        kernel,
        out_shape=jax.ShapeDtypeStruct((TILE, TILE), jnp.float32),
        in_specs=[smem, smem, anywhere, anywhere, anywhere, anywhere],
        out_specs=vmem,
        scratch_shapes=[
            pltpu.VMEM((COLS, 2, TILE, RANK), half),
            pltpu.VMEM((2, COLS, TILE, RANK), half),
            pltpu.VMEM((ROWS, 2, STEP, LANES), half),
            pltpu.VMEM((COLS, 2, STEP, LANES), half),
            pltpu.VMEM((TILE, TILE), half),
            pltpu.VMEM((TILE, RANK), half),
            pltpu.VMEM((TILE, TILE), half),
            sems((4,)),
            sems((2,)),
            sems((2,)),
            sems((2,)),
            sems((2, 14)),
            sems((2, 2, 2)),
            sems((2, 2, GROUPS[0][1], 4)),
            sems((2, 2, 2, 12)),
            sems((2, 2, 2, 4)),
        ],
        compiler_params=pltpu.CompilerParams(
            collective_id=0, has_side_effects=True, vmem_limit_bytes=60 * 2**20
        ),
    )(col_rows, ranks, trailing, u_factor, w_factor, diag_inverse)


def solution(mesh):
    placed = (
        P("row", "col"),
        P("row", "col", None, None),
        P("row", "col", None, None),
        P("col", None, None),
        P("row", "col"),
        P(),
    )
    return jax.shard_map(
        local, mesh=mesh, in_specs=placed, out_specs=P("row", "col"), check_vma=False
    )
```

time: 714 us -> 83.2 us (0.12)
  the two profiles are of different devices: /device:TPU:20 before, /device:TPU:1 now
where the time goes in v3:
time: 83.2 us; the launch traced here: 82 us
  Pallas kernels  79.1 us (95%)
  local copies, waits for them, and re-layouts  2.26 us (3%)
    pallas_call x1, Pallas kernels, local(): pl.pallas_call(kernel, out_shape=jax.ShapeDtypeStruct((TILE, TILE), jnp.f...  79.1 us
    unnamed x1, local copies, waits for them, and re-layouts  2.26 us

profile of v3, /device:TPU:1, one launch (start us, length us, event | category | flops | bytes accessed | tf_op | source)
XLA Modules:
  0.0 82.0 jit_solution(11617210547498716481)
XLA Ops:
  0.7 79.1 %shard_map.64 = f32[512,512]{1,0:T(8,128)} custom-call(s32[8]{0:T(128)} %pairs.1, s32[1,1]{1,0:T(1,128)S(6)} %copy.8.ranks, bf16[512,512]{1,0:T(8,128)(2,1)} %trailing.1, bf16[1,1,512,256]{3,2,1,0:T(8,128)(2,1)} %u_ref.1, bf16[1,1,512,256]{3,2,1,0:T(8,128)(2,1)} %w_ref.1, bf16[1,512,512]{2,1,0:T(8,128)(2,1)} %inverse_ref.1), custom_call_target="tpu_custom_call" | custom-call | tf_op jit(solution)/shard_map/pallas_call | solution.py:325
  79.7 2.3 %copy.9 = f32[512,512]{1,0:T(8,128)} copy(f32[512,512]{1,0:T(8,128)} %shard_map.64) | data formatting | bytes 2097152

commit v4 on v3

--- a/solution.py
+++ b/solution.py
@@ -15,15 +15,15 @@
 WAYS = (0, 1)
 GROUPS = ((0, 3), (3, 2), (5, 3))
 PLAN = (
-    0, 1, 3, 5, 5, 1, 1, 3, 3, 0, 2, 4, 1, 1, 2, 2, 3, 3, 5, 5, 4, 0, 0, 4, 0, 0, 0, 0, 2, 1, 1, 2,
-    3, 3, 4, 0, 0, 4, 0, 0, 2, 0, 0, 2, 1, 3, 5, 5, 4, 0, 0, 4, 0, 0, 0, 0, 2, 4, 5, 0, 2, 4,
+    0, 1, 3, 1, 1, 5, 5, 3, 3, 0, 2, 4, 1, 1, 2, 2, 3, 3, 4, 0, 0, 4, 0, 0, 0, 0, 2, 1, 1, 2, 3, 3,
+    4, 0, 0, 4, 0, 0, 2, 0, 0, 2, 1, 3, 4, 0, 0, 4, 0, 5, 5, 0, 0, 0, 2, 4, 0, 2, 4,
 )
 ORDER = [(0, 0)] + [(w, s) for s in (1, 2, 3) for w in WAYS] + [(0, 4)]
 
 
 def kernel(
     pairs, ranks, trailing, u_ref, w_ref, inverse_ref, out,
-    mine, theirs, landed, picked, base, w, inverse,
+    mine, factors, turned, theirs, landed, picked, mixed, base, w, inverse,
     load_sems, own_sems, spread_sems, place_sems, ring_sems,
     x_sems, z_sems, wide_x_sems, wide_z_sems,
 ):
@@ -41,7 +41,8 @@
         for i, (source, target) in enumerate((
             (inverse_ref.at[0], inverse),
             (w_ref.at[0, 0], w),
-            (u_ref.at[0, 0], mine.at[col, 1]),
+            (u_ref.at[0, 0], mine.at[1]),
+            (u_ref.at[0, 0], factors.at[col]),
             (trailing, base),
         ))
     ]
@@ -64,8 +65,11 @@
     loads[1].wait()
     product = jnp.dot(inverse[...], w[...], preferred_element_type=jnp.float32)
     lane = lax.broadcasted_iota(jnp.int32, (TILE, RANK), 1)
-    mine[col, 0] = jnp.where(lane < ranks[0, 0], product, 0.0).astype(jnp.bfloat16)
+    solved = jnp.where(lane < ranks[0, 0], product, 0.0)
+    mine[0] = solved.astype(jnp.bfloat16)
+    turned[col] = solved.T.astype(jnp.bfloat16)
     loads[2].wait()
+    loads[3].wait()
 
     pl.semaphore_wait(barrier, ROWS - 1 + 2 * (COLS - 1))
 
@@ -86,7 +90,7 @@
         place = (other // (NX * NY)) * NX + other % NX
         first = pl.multiple_of((other // NX) % NY * LANES, LANES)
         return mine.at[
-            col, :, pl.ds(pl.multiple_of(place * STEP, STEP), STEP), pl.ds(first, LANES)
+            :, pl.ds(pl.multiple_of(place * STEP, STEP), STEP), pl.ds(first, LANES)
         ]
 
     own = pltpu.make_async_copy(piece(row), landed.at[row], own_sems.at[0])
@@ -105,13 +109,20 @@
     across, twin = ((h + 2) % NH) * 2 + core, col + 1 - 2 * core
     count = [0]
 
-    def pass_on(panel, part, to, slot):
-        ref = mine.at[panel, part]
+    def row_factor(panel, part, quarter=None):
+        ref = turned.at[panel] if part == 0 else factors.at[panel]
+        if quarter is None:
+            return ref
+        height = ref.shape[0] // 4
+        return ref.at[pl.ds(0, height)] if quarter == 0 else ref.at[pl.ds(height, 3 * height)]
+
+    def pass_on(panel, part, to, slot, quarter=None):
+        ref = row_factor(panel, part, quarter)
         send(ref, ref, ring_sems.at[0, count[0]], ring_sems.at[1, slot], row, to)
         count[0] += 1
 
-    def ring_arrived(panel, part, slot):
-        arrived(mine.at[panel, part], ring_sems.at[1, slot])
+    def ring_arrived(panel, part, slot, quarter=None):
+        arrived(row_factor(panel, part, quarter), ring_sems.at[1, slot])
 
     pass_on(col, 0, right, 0)
     pass_on(col, 1, left, 3)
@@ -140,10 +151,12 @@
     place(partner, col)
     stay = pltpu.make_async_copy(picked.at[col], spot, own_sems.at[1])
     stay.start()
-    pass_on(col, 1, right, 1)
-    pass_on(col, 0, left, 2)
+    pass_on(col, 1, right, 14, 0)
+    pass_on(col, 0, left, 15, 0)
     stay.wait()
     arrived(landed.at[pl.ds(0, 2 * COLS - 1)], place_sems.at[1])
+    pass_on(col, 1, right, 1, 1)
+    pass_on(col, 0, left, 2, 1)
 
     x_side = (at(z, y, (x + 1) % NX), at(z, y, (x + NX - 1) % NX))
     z_side = (at((z + 1) % NZ, y, x), at((z + NZ - 1) % NZ, y, x))
@@ -269,48 +282,49 @@
         pass_on(col, 0, twin, 6)
         pass_on(col, 1, twin, 7)
         pass_on(left, 0, twin, 8)
-        ring_arrived(left, 1, 1)
+        ring_arrived(left, 1, 14, 0)
+        ring_arrived(left, 1, 1, 1)
         pass_on(left, 1, twin, 9)
 
     def cross_right():
         pass_on(right, 1, twin, 11)
-        ring_arrived(right, 0, 2)
+        ring_arrived(right, 0, 15, 0)
+        ring_arrived(right, 0, 2, 1)
         pass_on(right, 0, twin, 10)
 
-    def ring_end():
-        flip = 1 - 2 * core
-        for panel, slot in ((twin, 6), (left + flip, 8), (right + flip, 10), (across + flip, 12)):
-            ring_arrived(panel, 0, slot)
-            ring_arrived(panel, 1, slot + 1)
-
-    ring = [
-        onward(left, 0, 0, right, 4), onward(right, 1, 3, left, 5), cross_left, cross_right,
-        onward(across, 0, 4, twin, 12), onward(across, 1, 5, twin, 13), ring_end,
-    ]
+    def crossed(panel, slot):
+        for part in (0, 1):
+            ring_arrived(panel, part, slot + part)
+
+    ring = [onward(left, 0, 0, right, 4), onward(right, 1, 3, left, 5), cross_left, cross_right]
     flows = [narrow(*GROUPS[0]), *wide(0, *GROUPS[1]), *wide(1, *GROUPS[2]), ring]
     flows = [iter(flow) for flow in flows]
 
-    def work(first, size):
-        @pl.loop(first, first + size)
-        def _(k):
-            middle = lax.dot_general(
-                mine[k, 0], theirs[0, k], (((0,), (0,)), ((), ())),
-                preferred_element_type=jnp.float32,
-            ).astype(jnp.bfloat16)
-            mixed = jnp.dot(
-                mine[k, 1], middle, preferred_element_type=jnp.float32
-            ).astype(jnp.bfloat16)
-            out[...] -= lax.dot_general(
-                mixed, theirs[1, k], (((1,), (1,)), ((), ())), preferred_element_type=jnp.float32
-            )
-
-    for flow in PLAN[:-1]:
+    def work(*stops):
+        panels = [2 * ((h + stop) % NH) + i for stop in stops for i in (0, 1)]
+        for k in panels:
+            middle = jnp.dot(turned[k], theirs[0, k], preferred_element_type=jnp.float32)
+            middle = middle.astype(jnp.bfloat16)
+            product = jnp.dot(factors[k], middle, preferred_element_type=jnp.float32)
+            mixed[k] = product.astype(jnp.bfloat16)
+        rows = jnp.concatenate([mixed[k] for k in panels], axis=1)
+        cols = jnp.concatenate([theirs[1, k] for k in panels], axis=1)
+        return lax.dot_general(
+            rows, cols, (((1,), (1,)), ((), ())), preferred_element_type=jnp.float32
+        )
+
+    for flow in PLAN:
         next(flows[flow])()
-    loads[3].wait()
-    out[...] = base[...].astype(jnp.float32)
-    work(0, GROUPS[2][0])
-    next(flows[PLAN[-1]])()
-    work(*GROUPS[2])
+    flip = 1 - 2 * core
+    onward(across, 0, 4, twin, 12)()
+    onward(across, 1, 5, twin, 13)()
+    crossed(twin, 6)
+    crossed(left + flip, 8)
+    crossed(right + flip, 10)
+    loads[4].wait()
+    out[...] = base[...].astype(jnp.float32) - work(0, 1, 3)
+    crossed(across + flip, 12)
+    out[...] -= work(2)
 
     for copy in sent:
         copy.wait_send()
@@ -328,18 +342,21 @@
         in_specs=[smem, smem, anywhere, anywhere, anywhere, anywhere],
         out_specs=vmem,
         scratch_shapes=[
-            pltpu.VMEM((COLS, 2, TILE, RANK), half),
+            pltpu.VMEM((2, TILE, RANK), half),
+            pltpu.VMEM((COLS, TILE, RANK), half),
+            pltpu.VMEM((COLS, RANK, TILE), half),
             pltpu.VMEM((2, COLS, TILE, RANK), half),
             pltpu.VMEM((ROWS, 2, STEP, LANES), half),
             pltpu.VMEM((COLS, 2, STEP, LANES), half),
+            pltpu.VMEM((COLS, TILE, RANK), half),
             pltpu.VMEM((TILE, TILE), half),
             pltpu.VMEM((TILE, RANK), half),
             pltpu.VMEM((TILE, TILE), half),
-            sems((4,)),
+            sems((5,)),
             sems((2,)),
             sems((2,)),
             sems((2,)),
-            sems((2, 14)),
+            sems((2, 16)),
             sems((2, 2, 2)),
             sems((2, 2, GROUPS[0][1], 4)),
             sems((2, 2, 2, 12)),

time: 83.2 us -> 78.2 us (0.940); the launches traced: 82 us -> 78 us
  Pallas kernels: 79.1 us -> 75.1 us
    pallas_call x1, Pallas kernels: 79.1 us -> 75.1 us  [local(): pl.pallas_call(kernel, out_shape=jax.ShapeDtypeStruct((TILE, TILE), jnp.f...]
where the time goes in v4:
time: 78.2 us; the launch traced here: 78 us
  Pallas kernels  75.1 us (96%)
  local copies, waits for them, and re-layouts  2.26 us (3%)
    pallas_call x1, Pallas kernels, local(): pl.pallas_call(kernel, out_shape=jax.ShapeDtypeStruct((TILE, TILE), jnp.f...  75.1 us
    unnamed x1, local copies, waits for them, and re-layouts  2.26 us

profile of v4, /device:TPU:1, one launch (start us, length us, event | category | flops | bytes accessed | tf_op | source)
XLA Modules:
  0.0 78.0 jit_solution(5234646474293501827)
XLA Ops:
  0.7 75.1 %shard_map.64 = f32[512,512]{1,0:T(8,128)} custom-call(s32[8]{0:T(128)} %pairs.1, s32[1,1]{1,0:T(1,128)S(6)} %copy.8.ranks, bf16[512,512]{1,0:T(8,128)(2,1)} %trailing.1, bf16[1,1,512,256]{3,2,1,0:T(8,128)(2,1)} %u_ref.1, bf16[1,1,512,256]{3,2,1,0:T(8,128)(2,1)} %w_ref.1, bf16[1,512,512]{2,1,0:T(8,128)(2,1)} %inverse_ref.1), custom_call_target="tpu_custom_call" | custom-call | tf_op jit(solution)/shard_map/pallas_call | solution.py:339
  75.7 2.3 %copy.9 = f32[512,512]{1,0:T(8,128)} copy(f32[512,512]{1,0:T(8,128)} %shard_map.64) | data formatting | bytes 2097152

commit v5 on v4

--- a/solution.py
+++ b/solution.py
@@ -96,14 +96,18 @@
     own = pltpu.make_async_copy(piece(row), landed.at[row], own_sems.at[0])
     own.start()
 
-    @pl.loop(1, ROWS)
-    def _(d):
-        other = (row + d) % ROWS
+    def spread(up, across_plane):
+        other = at((z + up) % NZ, (y + across_plane // NX) % NY, (x + across_plane) % NX)
         pltpu.make_async_remote_copy(
             src_ref=piece(other), dst_ref=landed.at[row],
             send_sem=spread_sems.at[0], recv_sem=spread_sems.at[1],
             device_id=(other, col), device_id_type=MESH,
         ).start()
+
+    for up in (4, 3, 5, 2, 6, 1, 7, 0):
+        @pl.loop(1 if up == 0 else 0, NX * NY)
+        def _(d):
+            spread(up, d)
 
     right, left = ((h + 1) % NH) * 2 + core, ((h + NH - 1) % NH) * 2 + core
     across, twin = ((h + 2) % NH) * 2 + core, col + 1 - 2 * core
@@ -143,18 +147,17 @@
             device_id=(to_row, to_col), device_id_type=MESH,
         ).start()
 
-    @pl.loop(1, COLS)
-    def _(d):
+    for d in (4, 3, 5, 2, 6, 1, 7):
         place(row, (col + d) % COLS)
         place(partner, (col + d) % COLS)
 
     place(partner, col)
     stay = pltpu.make_async_copy(picked.at[col], spot, own_sems.at[1])
     stay.start()
+    stay.wait()
+    arrived(landed.at[pl.ds(0, 2 * COLS - 1)], place_sems.at[1])
     pass_on(col, 1, right, 14, 0)
     pass_on(col, 0, left, 15, 0)
-    stay.wait()
-    arrived(landed.at[pl.ds(0, 2 * COLS - 1)], place_sems.at[1])
     pass_on(col, 1, right, 1, 1)
     pass_on(col, 0, left, 2, 1)
 

time: 78.2 us -> 75.9 us (0.971)
  Pallas kernels: 75.1 us -> 72.8 us
    pallas_call x1, Pallas kernels: 75.1 us -> 72.8 us  [local(): pl.pallas_call(kernel, out_shape=jax.ShapeDtypeStruct((TILE, TILE), jnp.f...]
where the time goes in v5:
time: 75.9 us; the launch traced here: 75.7 us
  Pallas kernels  72.8 us (96%)
  local copies, waits for them, and re-layouts  2.26 us (3%)
    pallas_call x1, Pallas kernels, local(): pl.pallas_call(kernel, out_shape=jax.ShapeDtypeStruct((TILE, TILE), jnp.f...  72.8 us
    unnamed x1, local copies, waits for them, and re-layouts  2.26 us

profile of v5, /device:TPU:1, one launch (start us, length us, event | category | flops | bytes accessed | tf_op | source)
XLA Modules:
  0.0 75.7 jit_solution(4318646671373286399)
XLA Ops:
  0.7 72.8 %shard_map.64 = f32[512,512]{1,0:T(8,128)} custom-call(s32[8]{0:T(128)} %pairs.1, s32[1,1]{1,0:T(1,128)S(6)} %copy.8.ranks, bf16[512,512]{1,0:T(8,128)(2,1)} %trailing.1, bf16[1,1,512,256]{3,2,1,0:T(8,128)(2,1)} %u_ref.1, bf16[1,1,512,256]{3,2,1,0:T(8,128)(2,1)} %w_ref.1, bf16[1,512,512]{2,1,0:T(8,128)(2,1)} %inverse_ref.1), custom_call_target="tpu_custom_call" | custom-call | tf_op jit(solution)/shard_map/pallas_call | solution.py:342
  73.5 2.3 %copy.9 = f32[512,512]{1,0:T(8,128)} copy(f32[512,512]{1,0:T(8,128)} %shard_map.64) | data formatting | bytes 2097152

commit v6 on v5

--- a/solution.py
+++ b/solution.py
@@ -319,13 +319,14 @@
     for flow in PLAN:
         next(flows[flow])()
     flip = 1 - 2 * core
+    crossed(twin, 6)
+    crossed(right + flip, 10)
+    loads[4].wait()
+    out[...] = base[...].astype(jnp.float32) - work(0, 1)
     onward(across, 0, 4, twin, 12)()
     onward(across, 1, 5, twin, 13)()
-    crossed(twin, 6)
     crossed(left + flip, 8)
-    crossed(right + flip, 10)
-    loads[4].wait()
-    out[...] = base[...].astype(jnp.float32) - work(0, 1, 3)
+    out[...] -= work(3)
     crossed(across + flip, 12)
     out[...] -= work(2)
 

time: 75.9 us -> 77.5 us (1.021)
  Pallas kernels: 72.8 us -> 74.4 us
    pallas_call x1, Pallas kernels: 72.8 us -> 74.4 us  [local(): pl.pallas_call(kernel, out_shape=jax.ShapeDtypeStruct((TILE, TILE), jnp.f...]
where the time goes in v6:
time: 77.5 us; the launch traced here: 77.3 us
  Pallas kernels  74.4 us (96%)
  local copies, waits for them, and re-layouts  2.26 us (3%)
    pallas_call x1, Pallas kernels, local(): pl.pallas_call(kernel, out_shape=jax.ShapeDtypeStruct((TILE, TILE), jnp.f...  74.4 us
    unnamed x1, local copies, waits for them, and re-layouts  2.26 us

profile of v6, /device:TPU:1, one launch (start us, length us, event | category | flops | bytes accessed | tf_op | source)
XLA Modules:
  0.0 77.3 jit_solution(14878714709542574946)
XLA Ops:
  0.7 74.4 %shard_map.64 = f32[512,512]{1,0:T(8,128)} custom-call(s32[8]{0:T(128)} %pairs.1, s32[1,1]{1,0:T(1,128)S(6)} %copy.8.ranks, bf16[512,512]{1,0:T(8,128)(2,1)} %trailing.1, bf16[1,1,512,256]{3,2,1,0:T(8,128)(2,1)} %u_ref.1, bf16[1,1,512,256]{3,2,1,0:T(8,128)(2,1)} %w_ref.1, bf16[1,512,512]{2,1,0:T(8,128)(2,1)} %inverse_ref.1), custom_call_target="tpu_custom_call" | custom-call | tf_op jit(solution)/shard_map/pallas_call | solution.py:343
  75.1 2.3 %copy.9 = f32[512,512]{1,0:T(8,128)} copy(f32[512,512]{1,0:T(8,128)} %shard_map.64) | data formatting | bytes 2097152
